TPU v7x, 256 devices: a whole 4x4x8 slice. The times are simulated.
256 devices in a mesh: xy: 32 (over z, x_lo, core), gz: 8 (over y, x_hi).
Axes of the slice: x: 4 (x_hi: 2, x_lo: 2; x = x_hi * 2 + x_lo), y: 4, z: 8, core: 2. Of those that a mesh axis runs over, the one named last changes fastest.
Arguments:
- file_data: float32 [512, 64, 8192], P('gz', None, 'xy')
- factor: float32 [512, 256], P('gz'), may hold values from -0.25 to 0.25
- block_owner: int32 [64], replicated, may hold values from 0 to 31, as said below
- block_offset: int32 [64], replicated, may hold values from 0 to 128, as said below
Outputs:
- gram: float32 [512, 512], P('gz')
- core: float32 [256, 64, 8192], P('gz', None, 'xy')
Inputs may be any that keep to these rules, and one draw needn't show every extreme that they name: `block_owner`: block b of device d (b = d * 2 + j) is owned by d - 1, d or d + 1 modulo 32. Every index of xy owns exactly 2 blocks. `block_offset`: offsets are multiples of 128; the blocks of one owner take distinct offsets, so every file slot is named once.
All inputs are finite; a program needn't handle non-finite values.
Results may differ from a plain program's by a relative error of at most 0.00007.
Values sent between devices are 32-bit elements; how exact they have to be, the bound alone decides.
A program may use at most 128 MiB of HBM per device.

v0:
```python
import jax
import jax.numpy as jnp
from jax import lax
from jax.sharding import PartitionSpec as P

BLOCKS_DEV = 2


def shifted(array, axis, by):
    length = lax.axis_size(axis)
    return lax.ppermute(array, axis, [(i, (i + by) % length) for i in range(length)])


def take_block(buffer, offset):
    return lax.dynamic_slice_in_dim(buffer, offset, 128, 2)


def rebalance(buffer, block_owner, block_offset):
    devices = lax.axis_size("xy")
    myself = lax.axis_index("xy")
    lower_peer = (myself + devices - 1) % devices
    upper_peer = (myself + 1) % devices

    def outgoing(target):
        pieces = []
        for j in range(BLOCKS_DEV):
            pieces.append(take_block(buffer, block_offset[target * BLOCKS_DEV + j]))
        return jnp.concatenate(pieces, axis=2)

    from_lower = shifted(outgoing(upper_peer), "xy", 1)
    from_upper = shifted(outgoing(lower_peer), "xy", -1)
    blocks = []
    for j in range(BLOCKS_DEV):
        owner = block_owner[myself * BLOCKS_DEV + j]
        offset = block_offset[myself * BLOCKS_DEV + j]
        local_block = take_block(buffer, offset)
        lower_block = from_lower[:, :, j * 128 : (j + 1) * 128]
        upper_block = from_upper[:, :, j * 128 : (j + 1) * 128]
        remote = jnp.where(owner == lower_peer, lower_block, upper_block)
        blocks.append(jnp.where(owner == myself, local_block, remote))
    return jnp.concatenate(blocks, axis=2)


def halves(x):
    high = lax.reduce_precision(x, exponent_bits=8, mantissa_bits=7)
    low = x - high
    return (high.astype(jnp.bfloat16), low.astype(jnp.bfloat16))


def dot(spec, a, b):
    return jnp.einsum(spec, a, b, preferred_element_type=jnp.float32)


def local(file_data, factor, block_owner, block_offset):
    whole_factor = lax.all_gather(factor, "gz", axis=0, tiled=True)
    swapped = lax.all_to_all(file_data, "gz", split_axis=1, concat_axis=0, tiled=True)
    scale = 1.0 / (BLOCKS_DEV * 128 * lax.axis_size("xy") * file_data.shape[1])
    high, low = halves(swapped)
    factor_high, factor_low = halves(whole_factor)
    core_part = (
        dot("zr,zcs->rcs", factor_high, high)
        + dot("zr,zcs->rcs", factor_high, low)
        + dot("zr,zcs->rcs", factor_low, high)
    )
    core = lax.all_to_all(core_part, "gz", split_axis=0, concat_axis=1, tiled=True)
    cross = dot("zcs,wcs->zw", high, low)
    partial_gram = (dot("zcs,wcs->zw", high, high) + (cross + cross.T)) * scale
    gram = lax.psum_scatter(partial_gram, "gz", scatter_dimension=0, tiled=True)
    gram = lax.psum(gram, "xy")
    core = rebalance(core, block_owner, block_offset)
    return (gram, core)


def solution(mesh):
    return jax.shard_map(
        local,
        mesh=mesh,
        in_specs=(P("gz", None, "xy"), P("gz", None), P(), P()),
        out_specs=(P("gz", None), P("gz", None, "xy")),
        check_vma=False,
    )
```

profile of v0, /device:TPU:4, one launch (start us, length us, event | category | flops | bytes accessed | tf_op | source)
XLA Modules:
  0.0 449.4 jit_solution(16877087336601075316)
XLA Ops:
  7.2 6.6 %copy.13 = f32[64,64,256]{2,0,1:T(8,128)} copy(f32[64,64,256]{2,1,0:T(8,128)} %param.4) | data formatting | bytes 8388608 | tf_op args[0]
  13.8 7.6 %all-to-all-start = ((f32[64,64,256]{2,0,1:T(8,128)}), f32[64,64,256]{2,0,1:T(8,128)}, u32[]{:S(2)}, u32[]{:S(2)}) async-start(f32[64,64,256]{2,0,1:T(8,128)} %copy.13), calls=%async_computation | async-start | bytes 8388608 | tf_op jit(solution)/shard_map/all_to_all | solution.py:56
  21.3 74.6 %all_gather.3 = f32[512,256]{1,0:T(8,128)S(1)} all-gather(f32[64,256]{1,0:T(8,128)S(1)} %copy-done.2), channel_id=1, replica_groups=mesh['xy'=32,'gz'=8] {'gz'}, dimensions={0}, use_global_device_ids=true | all-gather | bytes 589824 | tf_op jit(solution)/shard_map/all_gather | solution.py:55
  96.2 2.5 copy.14
  98.6 1.0 fusion.1
  100.4 0.7 fusion.13
  101.1 0.8 fusion.2
  101.9 2.6 copy.21
  104.5 8.9 %all-to-all-start.1 = ((f32[256,8,256]{2,1,0:T(8,128)}), f32[256,8,256]{2,1,0:T(8,128)S(1)}, u32[]{:S(2)}, u32[]{:S(2)}) async-start(f32[256,8,256]{2,1,0:T(8,128)} %copy.21), calls=%async_computation.2 | async-start | bytes 4194304 | tf_op jit(solution)/shard_map/all_to_all | solution.py:65
  121.5 3.1 fusion
  124.7 1.3 copy-done.1
  126.0 1.3 convolution_bitcast_fusion
  127.3 1.3 copy.15
  128.6 4.8 %fusion.4 = f32[512,512]{1,0:T(8,128)} fusion(bf16[512,8,256]{2,0,1:T(8,128)(2,1)} %bitcast.59, f32[512,512]{1,0:T(8,128)S(1)} %convolution_bitcast_fusion, f32[512,512]{0,1:T(8,128)} %copy.15), kind=kOutput, calls=%fused_computation.15 | convolution fusion | flops 1074528256 | bytes 5242880 | tf_op jit(solution)/shard_map/zcs,wcs->zw/dot_general | solution.py:51
  133.5 1.3 copy-done
  134.8 1.9 copy.30
  136.6 1.2 constant_dynamic-slice_fusion.3
  137.8 1.5 pad_maximum_fusion.1
  139.3 1.5 pad_maximum_fusion
  147.6 85.8 %reduce-scatter.2.cloned.1.call-done = f32[64,512]{1,0:T(8,128)} async-done(((f32[512,512]{1,0:T(8,128)}), f32[64,512]{1,0:T(8,128)}) %reduce-scatter.2.cloned.1.call-update) | async-done | bytes 131088 | tf_op jit(solution)/shard_map/reduce_scatter | solution.py:68
  233.5 2.9 fusion.6
  236.4 1.5 pad_maximum_fusion.2
  237.9 203.1 %all-reduce.2.cloned.1.call-done = f32[64,512]{1,0:T(8,128)} async-done(((f32[64,512]{1,0:T(8,128)}), f32[64,512]{1,0:T(8,128)}) %all-reduce.2.cloned.1.call-update) | async-done | bytes 131088 | tf_op jit(solution)/shard_map/psum | solution.py:69
  441.0 1.6 copy.32
  (21 shorter events, 2.2 us)
Async XLA Ops:
  13.8 7.6 %copy-start.2 = (f32[64,256]{1,0:T(8,128)S(1)}, f32[64,256]{1,0:T(8,128)}, u32[]{:S(2)}) copy-start(f32[64,256]{1,0:T(8,128)} %param.5) | copy-start | bytes 196612
  13.8 82.4 %all-to-all-start = ((f32[64,64,256]{2,0,1:T(8,128)}), f32[64,64,256]{2,0,1:T(8,128)}, u32[]{:S(2)}, u32[]{:S(2)}) async-start(f32[64,64,256]{2,0,1:T(8,128)} %copy.13), calls=%async_computation | async-start | bytes 8388608 | tf_op jit(solution)/shard_map/all_to_all | solution.py:56
  104.5 8.9 %copy-start.3 = (s32[64]{0:T(128)S(1)}, s32[64]{0:T(128)}, u32[]{:S(2)}) copy-start(s32[64]{0:T(128)} %param.7) | copy-start | bytes 772
  104.5 8.9 %copy-start.4 = (s32[64]{0:T(128)S(1)}, s32[64]{0:T(128)}, u32[]{:S(2)}) copy-start(s32[64]{0:T(128)} %param.6) | copy-start | bytes 772
  104.5 29.0 %all-to-all-start.1 = ((f32[256,8,256]{2,1,0:T(8,128)}), f32[256,8,256]{2,1,0:T(8,128)S(1)}, u32[]{:S(2)}, u32[]{:S(2)}) async-start(f32[256,8,256]{2,1,0:T(8,128)} %copy.21), calls=%async_computation.2 | async-start | bytes 4194304 | tf_op jit(solution)/shard_map/all_to_all | solution.py:65
  113.4 120.0 %reduce-scatter.2.cloned.1.call-start = ((), (), s32[]{:S(2)}) async-start(), calls=%async_computation.3 | async-start | bytes 1179648 | tf_op jit(solution)/shard_map/reduce_scatter | solution.py:68
  124.7 1.3 copy-start.1
  133.4 307.6 %all-reduce.2.cloned.1.call-start = ((), (), s32[]{:S(2)}) async-start(), calls=%async_computation.4 | async-start | bytes 262144 | tf_op jit(solution)/shard_map/psum | solution.py:69
  133.4 1.3 copy-start
  139.3 94.2 %collective-permute-start.1 = (f32[32,64,256]{2,1,0:T(8,128)}, f32[32,64,256]{2,1,0:T(8,128)}, u32[]{:S(2)}, u32[]{:S(2)}) collective-permute-start(f32[32,64,256]{2,1,0:T(8,128)} %pad_maximum_fusion.1), channel_id=1, source_target_pairs={{0,248},{8,0},{16,8},{24,16},{32,24},{40,32},{48,40},{56,48},{64,5... | collective-permute-start | bytes 6291464 | tf_op jit(solution)/shard_map/ppermute | solution.py:11
  140.8 92.6 %collective-permute-start = (f32[32,64,256]{2,1,0:T(8,128)}, f32[32,64,256]{2,1,0:T(8,128)}, u32[]{:S(2)}, u32[]{:S(2)}) collective-permute-start(f32[32,64,256]{2,1,0:T(8,128)} %pad_maximum_fusion), channel_id=1, source_target_pairs={{0,8},{8,16},{16,24},{24,32},{32,40},{40,48},{48,56},{56,64},{64,7... | collective-permute-start | bytes 6291464 | tf_op jit(solution)/shard_map/ppermute | solution.py:11
Sparse Core Ops, SparseCore 0:
  133.5 99.8 reduce-scatter.1
  236.0 204.9 all-reduce.1
where the time goes:
time: 450 us; the launch traced here: 449 us
  waiting for transfers between devices  289 us (64%)
  blocking collectives  74.6 us (17%)
  between operations  27.9 us (6%)
  local copies, waits for them, and re-layouts  21.1 us (5%)
  starting transfers between devices  17 us (4%)
  other arithmetic  11.6 us (3%)
  matrix products  8.25 us (2%)
    psum x1, waiting for transfers between devices, local(): gram = lax.psum(gram, 'xy')  203 us
    reduce_scatter x1, waiting for transfers between devices, local(): gram = lax.psum_scatter(partial_gram, 'gz', scatter_dimension=0, tiled=True)  85.8 us
    all_gather x1, blocking collectives, local(): whole_factor = lax.all_gather(factor, 'gz', axis=0, tiled=True)  74.6 us
    unnamed x12, local copies, waits for them, and re-layouts  10.8 us
  transfers between devices with their start and end apart: 6, of which 2 were waited for; matrix products, arithmetic and copies ran while one was open for 5% of the time, Pallas kernels for 0%

commit v1 on v0

--- a/solution.py
+++ b/solution.py
@@ -66,7 +66,7 @@
     cross = dot("zcs,wcs->zw", high, low)
     partial_gram = (dot("zcs,wcs->zw", high, high) + (cross + cross.T)) * scale
     gram = lax.psum_scatter(partial_gram, "gz", scatter_dimension=0, tiled=True)
-    gram = lax.psum(gram, "xy")
+    gram = lax.all_gather(gram, axis_name="xy").sum(axis=0)
     core = rebalance(core, block_owner, block_offset)
     return (gram, core)
 

time: 450 us -> 303 us (0.67)
  the two profiles are of different devices: /device:TPU:4 before, /device:TPU:1 now
where the time goes in v1:
time: 303 us; the launch traced here: 302 us
  waiting for transfers between devices  138 us (46%)
  blocking collectives  88.5 us (29%)
  between operations  27.6 us (9%)
  local copies, waits for them, and re-layouts  17.4 us (6%)
  other arithmetic  12.4 us (4%)
  starting transfers between devices  11.1 us (4%)
  matrix products  6.99 us (2%)
    reduce_scatter x1, waiting for transfers between devices, local(): gram = lax.psum_scatter(partial_gram, 'gz', scatter_dimension=0, tiled=True)  75.8 us
    all_to_all x1, blocking collectives, local(): lax.all_to_all(file_data, 'gz', split_axis=1, concat_axis=0, tiled=True)  57.3 us
    ppermute x2, waiting for transfers between devices, shifted(): lax.ppermute(array, axis, [(i, (i + by) % length) for i in range(length)])  38.8 us
    all_gather x1, blocking collectives, local(): whole_factor = lax.all_gather(factor, 'gz', axis=0, tiled=True)  31.2 us
    all_to_all x1, waiting for transfers between devices, local(): lax.all_to_all(core_part, 'gz', split_axis=0, concat_axis=1, tiled=True)  23.4 us
    ppermute x2, starting transfers between devices, shifted(): lax.ppermute(array, axis, [(i, (i + by) % length) for i in range(length)])  7.28 us
    unnamed x11, local copies, waits for them, and re-layouts  7.12 us
    dot_general x5, matrix products, dot(): return jnp.einsum(spec, a, b, preferred_element_type=jnp.float32)  6.99 us
  transfers between devices with their start and end apart: 5, of which 3 were waited for; matrix products, arithmetic and copies ran while one was open for 6% of the time, Pallas kernels for 0%

profile of v1, /device:TPU:1, one launch (start us, length us, event | category | flops | bytes accessed | tf_op | source)
XLA Modules:
  0.0 302.1 jit_solution(1193531740150147953)
XLA Ops:
  7.2 4.6 %copy.13 = f32[64,64,256]{2,0,1:T(8,128)S(1)} copy(f32[64,64,256]{2,1,0:T(8,128)} %param.4) | data formatting | bytes 8388608 | tf_op args[0]
  11.8 57.3 %all_to_all.36 = f32[64,64,256]{2,0,1:T(8,128)S(1)} all-to-all(f32[64,64,256]{2,0,1:T(8,128)S(1)} %copy.13), channel_id=1, replica_groups=mesh['xy'=32,'gz'=8] {'gz'}, dimensions={1} | all-to-all | bytes 8388608 | tf_op jit(solution)/shard_map/all_to_all | solution.py:56
  70.0 1.2 copy-done
  71.1 1.3 convolution_bitcast_fusion
  72.4 1.3 copy.15
  73.7 3.5 %fusion.4 = f32[512,512]{1,0:T(8,128)} fusion(bf16[512,8,256]{2,0,1:T(8,128)(2,1)S(1)} %bitcast.63, f32[512,512]{1,0:T(8,128)S(1)} %convolution_bitcast_fusion, f32[512,512]{0,1:T(8,128)} %copy.15), kind=kOutput, calls=%fused_computation.15 | convolution fusion | flops 1074528256 | bytes 5242880 | tf_op jit(solution)/shard_map/zcs,wcs->zw/dot_general | solution.py:51
  77.3 75.8 %reduce-scatter.2.cloned.1.call-done = f32[64,512]{1,0:T(8,128)} async-done(((f32[512,512]{1,0:T(8,128)}), f32[64,512]{1,0:T(8,128)}) %reduce-scatter.2.cloned.1.call-update) | async-done | bytes 131088 | tf_op jit(solution)/shard_map/reduce_scatter | solution.py:68
  153.2 31.2 %all_gather.11 = f32[512,256]{1,0:T(8,128)S(1)} all-gather(f32[64,256]{1,0:T(8,128)S(1)} %copy-done.2), channel_id=1, replica_groups=mesh['xy'=32,'gz'=8] {'gz'}, dimensions={0}, use_global_device_ids=true | all-gather | bytes 589824 | tf_op jit(solution)/shard_map/all_gather | solution.py:55
  184.6 2.5 copy.14
  187.0 1.0 fusion.1
  190.3 2.5 copy.21
  192.9 3.7 %all-to-all-start.1 = ((f32[256,8,256]{2,1,0:T(8,128)}), f32[256,8,256]{2,1,0:T(8,128)S(1)}, u32[]{:S(2)}, u32[]{:S(2)}) async-start(f32[256,8,256]{2,1,0:T(8,128)} %copy.21), calls=%async_computation.2 | async-start | bytes 4194304 | tf_op jit(solution)/shard_map/all_to_all | solution.py:65
  204.7 23.4 %all-to-all-done.1 = f32[256,8,256]{2,1,0:T(8,128)S(1)} async-done(((f32[256,8,256]{2,1,0:T(8,128)}), f32[256,8,256]{2,1,0:T(8,128)S(1)}, u32[]{:S(2)}, u32[]{:S(2)}) %all-to-all-start.1) | async-done | bytes 2097184 | tf_op jit(solution)/shard_map/all_to_all | solution.py:65
  228.1 1.3 copy-done.1
  229.4 1.9 copy.30
  231.2 1.2 constant_dynamic-slice_fusion.3
  232.4 1.5 pad_maximum_fusion.1
  233.9 5.8 %collective-permute-start.1 = (f32[32,64,256]{2,1,0:T(8,128)}, f32[32,64,256]{2,1,0:T(8,128)}, u32[]{:S(2)}, u32[]{:S(2)}) collective-permute-start(f32[32,64,256]{2,1,0:T(8,128)} %pad_maximum_fusion.1), channel_id=1, source_target_pairs={{0,248},{8,0},{16,8},{24,16},{32,24},{40,32},{48,40},{56,48},{64,5... | collective-permute-start | bytes 6291464 | tf_op jit(solution)/shard_map/ppermute | solution.py:11
  239.7 1.5 pad_maximum_fusion
  241.2 1.5 collective-permute-start
  248.8 38.8 %collective-permute-done.1 = f32[32,64,256]{2,1,0:T(8,128)} collective-permute-done((f32[32,64,256]{2,1,0:T(8,128)}, f32[32,64,256]{2,1,0:T(8,128)}, u32[]{:S(2)}, u32[]{:S(2)}) %collective-permute-start.1) | collective-permute-done | bytes 2097184 | tf_op jit(solution)/shard_map/ppermute | solution.py:11
  287.7 2.9 fusion.6
  290.6 1.5 pad_maximum_fusion.2
  292.1 3.2 %reduce_sum.9 = f32[64,512]{1,0:T(8,128)} reduce(f32[32,64,512]{2,1,0:T(8,128)} %bitcast.61, f32[]{:T(128)} %constant.31.clone.1), dimensions={0}, to_apply=%region_1.0 | reduce | flops 1015808 | bytes 4325380 | tf_op jit(solution)/shard_map/reduce_sum | solution.py:69
  (20 shorter events, 4.0 us)
Async XLA Ops:
  7.2 146.0 %reduce-scatter.2.cloned.1.call-start = ((), (), s32[]{:S(2)}) async-start(), calls=%async_computation.3 | async-start | bytes 1179648 | tf_op jit(solution)/shard_map/reduce_scatter | solution.py:68
  69.2 2.0 copy-start
  73.7 79.5 %copy-start.2 = (f32[64,256]{1,0:T(8,128)S(1)}, f32[64,256]{1,0:T(8,128)}, u32[]{:S(2)}) copy-start(f32[64,256]{1,0:T(8,128)} %param.5) | copy-start | bytes 196612
  77.2 214.9 %all-gather.3.cloned.1.call-start = ((), (), s32[]{:S(2)}) async-start(), calls=%async_computation.4 | async-start | bytes 4325376 | tf_op jit(solution)/shard_map/all_gather | solution.py:69
  192.8 3.8 %copy-start.3 = (s32[64]{0:T(128)S(1)}, s32[64]{0:T(128)}, u32[]{:S(2)}) copy-start(s32[64]{0:T(128)} %param.7) | copy-start | bytes 772
  192.9 3.8 %copy-start.4 = (s32[64]{0:T(128)S(1)}, s32[64]{0:T(128)}, u32[]{:S(2)}) copy-start(s32[64]{0:T(128)} %param.6) | copy-start | bytes 772
  192.9 35.2 %all-to-all-start.1 = ((f32[256,8,256]{2,1,0:T(8,128)}), f32[256,8,256]{2,1,0:T(8,128)S(1)}, u32[]{:S(2)}, u32[]{:S(2)}) async-start(f32[256,8,256]{2,1,0:T(8,128)} %copy.21), calls=%async_computation.2 | async-start | bytes 4194304 | tf_op jit(solution)/shard_map/all_to_all | solution.py:65
  228.1 1.3 copy-start.1
  233.9 53.8 %collective-permute-start.1 = (f32[32,64,256]{2,1,0:T(8,128)}, f32[32,64,256]{2,1,0:T(8,128)}, u32[]{:S(2)}, u32[]{:S(2)}) collective-permute-start(f32[32,64,256]{2,1,0:T(8,128)} %pad_maximum_fusion.1), channel_id=1, source_target_pairs={{0,248},{8,0},{16,8},{24,16},{32,24},{40,32},{48,40},{56,48},{64,5... | collective-permute-start | bytes 6291464 | tf_op jit(solution)/shard_map/ppermute | solution.py:11
  241.2 46.5 %collective-permute-start = (f32[32,64,256]{2,1,0:T(8,128)}, f32[32,64,256]{2,1,0:T(8,128)}, u32[]{:S(2)}, u32[]{:S(2)}) collective-permute-start(f32[32,64,256]{2,1,0:T(8,128)} %pad_maximum_fusion), channel_id=1, source_target_pairs={{0,8},{8,16},{16,24},{24,32},{32,40},{40,48},{48,56},{56,64},{64,7... | collective-permute-start | bytes 6291464 | tf_op jit(solution)/shard_map/ppermute | solution.py:11
Sparse Core Ops, SparseCore 0:
  77.4 75.7 reduce-scatter.1
  155.0 68.0 all-gather.2
